TPU v7x, 128 devices: a whole 4x4x4 slice. The times are simulated.
128 devices in a mesh: grp: 4 (over z), dev: 32 (over x, y, core).
Axes of the slice: x: 4, y: 4, z: 4, core: 2. Of those that a mesh axis runs over, the one named last changes fastest.
Arguments:
- trace: bfloat16 [786432, 256], P(('grp', 'dev')), may hold values from -6 to 6
- counts: int32 [4, 32, 32], P('grp', 'dev'), may hold values from 1 to 192, as said below
Outputs:
- cross_corr: float32 [256, 128, 128], P(('grp', 'dev'))
Inputs may be any that keep to these rules, and one draw needn't show every extreme that they name: Every destination column counts[g, :, d] sums to 3072, and in every column one entry equals 192.
All inputs are finite; a program needn't handle non-finite values.
Results may differ from a plain program's by a relative error of at most 0.0003.
Values may be sent and summed in bfloat16 or wider, within the bound.
A program may use at most 128 MiB of HBM per device.

v0:
```python
import math

import jax
import jax.numpy as jnp
from jax import lax
from jax.sharding import PartitionSpec as P

NU = 128
NY = 128
LAGS = 256


def passed_along(value, axis, steps):
    count = lax.axis_size(axis)
    initial, last = (max(0, -steps), min(count, count - steps))
    return lax.ppermute(value, axis, [(source, source + steps) for source in range(initial, last)])


def per_device(trace, counts):
    dev_count = lax.axis_size("dev")
    group_count = lax.axis_size("grp")
    capacity = trace.shape[0]
    slot_rows = capacity // dev_count
    owned = capacity // 2
    send_counts = counts.reshape(-1)
    starts = jnp.cumsum(send_counts) - send_counts
    slot_ids = jnp.arange(slot_rows, dtype=jnp.int32)
    row_index = jnp.minimum(starts[:, None] + slot_ids[None, :], capacity - 1)
    live_rows = slot_ids[None, :] < send_counts[:, None]
    packed = jnp.where(live_rows[:, :, None], trace[row_index], jnp.zeros((), trace.dtype))
    received, recv_counts = (
        lax.all_to_all(packed, "dev", split_axis=0, concat_axis=0, tiled=True),
        lax.all_to_all(
            send_counts.reshape(dev_count, 1), "dev", split_axis=0, concat_axis=0, tiled=True
        ),
    )
    recv_counts = recv_counts.reshape(-1)
    offsets = jnp.cumsum(recv_counts) - recv_counts
    row_ids = jnp.arange(owned, dtype=jnp.int32)
    before = (offsets[None, :] <= row_ids[:, None]).astype(jnp.int32)
    source = jnp.sum(before, axis=1) - 1
    onehot = jnp.arange(dev_count, dtype=jnp.int32)[None, :] == source[:, None]
    first_row = jnp.sum(jnp.where(onehot, offsets[None, :], 0), axis=1)
    flat_index = source * slot_rows + row_ids - first_row
    window = received.reshape(dev_count * slot_rows, trace.shape[1])[flat_index]
    lag_count = LAGS
    preceding_rows = passed_along(window[owned - lag_count :, :NU], "dev", 1)
    power_rows = jnp.concatenate([preceding_rows, window[:, :NU]], axis=0)
    sensor = window[:, NU:]
    norm_scale = 1.0 / math.sqrt(group_count * dev_count * owned)
    block_width = 16

    def lag_block(block_id):
        first_lag = block_id * block_width
        begin = lag_count - first_lag - (block_width - 1)
        stretch = lax.dynamic_slice_in_dim(power_rows, begin, owned + block_width - 1, 0)
        stacked = jnp.concatenate(
            [
                stretch[block_width - 1 - step : block_width - 1 - step + owned]
                for step in range(block_width)
            ],
            axis=1,
        )
        product = lax.dot_general(
            sensor, stacked, (((0,), (0,)), ((), ())), preferred_element_type=jnp.float32
        )
        product = product.reshape(sensor.shape[1], block_width, NU)
        return jnp.transpose(product, (1, 0, 2)) * norm_scale

    all_terms = lax.map(lag_block, jnp.arange(lag_count // block_width, dtype=jnp.int32))
    all_terms = all_terms.reshape(lag_count, NY, NU)
    return lax.psum_scatter(all_terms, ("grp", "dev"), scatter_dimension=0, tiled=True)


def solution(mesh):
    in_specs = (P(("grp", "dev"), None), P("grp", "dev", None))
    out_specs = P(("grp", "dev"), None, None)
    return jax.shard_map(
        per_device, mesh=mesh, in_specs=in_specs, out_specs=out_specs, check_vma=False
    )
```

profile of v0, /device:TPU:0, one launch (start us, length us, event | category | flops | bytes accessed | tf_op | source)
XLA Modules:
  0.0 1624.0 jit_solution(16419179364117293816)
XLA Ops:
  8.0 7.4 all-to-all-start.1
  18.0 24.9 %gather_fusion = bf16[6144,256]{1,0:T(8,128)(2,1)} fusion(bf16[6144,256]{1,0:T(8,128)(2,1)S(1)} %copy-done, s32[6144]{0:T(1024)S(1)} %broadcast_clamp_fusion), kind=kCustom, calls=%fused_computation | custom fusion | bytes 6316032 | tf_op jit(solution)/shard_map/gather | solution.py:30
  42.9 4.9 broadcast_select_fusion
  47.8 7.5 all-to-all-start
  56.5 38.9 %all-to-all-done = bf16[32,192,256]{2,1,0:T(8,128)(2,1)} async-done(((bf16[32,192,256]{2,1,0:T(8,128)(2,1)}), bf16[32,192,256]{2,1,0:T(8,128)(2,1)}, u32[]{:S(2)}, u32[]{:S(2)}) %all-to-all-start) | async-done | bytes 3145760 | tf_op jit(solution)/shard_map/all_to_all | solution.py:32
  95.4 14.4 gather_fusion.1
  115.8 827.4 %while.14 = (s32[]{:T(128)}, f32[16,16,128,128]{3,2,1,0:T(8,128)}, s32[16]{0:T(128)S(1)}, bf16[3328,128]{1,0:T(8,128)(2,1)}, bf16[3072,128]{1,0:T(8,128)(2,1)}, ...) while((s32[]{:T(128)}, f32[16,16,128,128]{3,2,1,0:T(8,128)}, ...), condition=%wide.region_5.6_spmd, body=%wide.region_4.5_spmd.sunk | while | flops 1610874880 | bytes 43779096 | solution.py:70
  153.4 9.3 convolution_multiply_fusion.2
  162.6 2.6 copy.24
  205.1 9.3 convolution_multiply_fusion.2
  214.3 2.6 copy.24
  256.8 9.3 convolution_multiply_fusion.2
  266.1 2.6 copy.24
  308.5 9.3 convolution_multiply_fusion.2
  360.2 9.3 convolution_multiply_fusion.2
  369.5 2.6 copy.24
  411.9 9.3 convolution_multiply_fusion.2
  463.6 9.3 convolution_multiply_fusion.2
  472.9 2.6 copy.24
  515.3 9.3 convolution_multiply_fusion.2
  524.6 2.6 copy.24
  567.0 9.3 convolution_multiply_fusion.2
  618.8 9.3 convolution_multiply_fusion.2
  670.5 9.3 convolution_multiply_fusion.2
  722.2 9.3 convolution_multiply_fusion.2
  773.9 9.3 convolution_multiply_fusion.2
  783.1 2.6 copy.24
  825.6 9.3 convolution_multiply_fusion.2
  834.9 2.6 copy.24
  877.3 9.3 convolution_multiply_fusion.2
  929.0 9.3 convolution_multiply_fusion.2
  943.2 674.0 %reduce-scatter.2.cloned.1.call-done = f32[2,128,128]{2,1,0:T(8,128)} async-done(((f32[256,128,128]{2,1,0:T(8,128)}), f32[2,128,128]{2,1,0:T(8,128)}) %reduce-scatter.2.cloned.1.call-update) | async-done | bytes 131088 | tf_op jit(solution)/shard_map/reduce_scatter | solution.py:72
  (326 shorter events, 660.6 us)
Async XLA Ops:
  6.5 11.4 copy-start
  8.0 39.8 %all-to-all-start.1 = ((s32[32,1,1]{2,1,0:T(1,128)}), s32[32,1,1]{2,1,0:T(1,128)S(1)}, u32[]{:S(2)}, u32[]{:S(2)}) async-start(s32[32,1,1]{2,1,0:T(1,128)} %copy.18), calls=%async_computation.1 | async-start | bytes 32768 | tf_op jit(solution)/shard_map/all_to_all | solution.py:33
  47.8 47.7 %all-to-all-start = ((bf16[32,192,256]{2,1,0:T(8,128)(2,1)}), bf16[32,192,256]{2,1,0:T(8,128)(2,1)}, u32[]{:S(2)}, u32[]{:S(2)}) async-start(bf16[32,192,256]{2,1,0:T(8,128)(2,1)} %broadcast_select_fusion), calls=%async_computation | async-start | bytes 6291456 | tf_op jit(solution)/shard_map/all_to_all | solution.py:32
  55.3 1561.9 %reduce-scatter.2.cloned.1.call-start = ((), (), s32[]{:S(2)}) async-start(), calls=%async_computation.3 | async-start | bytes 16908288 | tf_op jit(solution)/shard_map/reduce_scatter | solution.py:72
  110.7 4.1 collective-permute-start
Sparse Core Ops, SparseCore 0:
  943.3 673.8 reduce-scatter.1
where the time goes:
time: 1640 us; the launch traced here: 1620 us
  local copies, waits for them, and re-layouts  715 us (44%)
  waiting for transfers between devices  713 us (43%)
  matrix products  148 us (9%)
  starting transfers between devices  16.7 us (1%)
    reduce_scatter x1, waiting for transfers between devices, per_device(): lax.psum_scatter(all_terms, ('grp', 'dev'), scatter_dimension=0, tiled=True)  674 us
    while x240, local copies, waits for them, and re-layouts  546 us
    dot_general x16, matrix products, lag_block(): lax.dot_general(sensor, stacked, (((0,), (0,)), ((), ())), preferred_elem...  148 us
    dynamic_update_slice x32, local copies, waits for them, and re-layouts, per_device(): lax.map(lag_block, jnp.arange(lag_count // block_width, dtype=jnp.int32))  78 us
    all_to_all x1, waiting for transfers between devices, per_device(): lax.all_to_all(packed, 'dev', split_axis=0, concat_axis=0, tiled=True)  38.9 us
    concatenate x16, local copies, waits for them, and re-layouts, lag_block(): jnp.concatenate([stretch[block_width - 1 - step:block_width - 1 - step +...  36.4 us
  transfers between devices with their start and end apart: 4, of which 2 were waited for; matrix products, arithmetic and copies ran while one was open for 2% of the time, Pallas kernels for 0%

commit v1 on v0

v1 whole, which is shorter than its diff:
```python
import functools
import math

import jax
import jax.numpy as jnp
from jax import lax
from jax.experimental import pallas as pl
from jax.experimental.pallas import tpu as pltpu
from jax.sharding import PartitionSpec as P

NU = 128
LAGS = 256
MESH = pl.DeviceIdType.MESH
DIMS = 6
BLOCKS = 64
HALO = 256
LEAD = 240
PARTS = (48, 40, 40, 48, 40, 40)
PART_AT = (0, 48, 88, 128, 176, 216)
K_CHUNK = 2048


def pack_kernel(per_step, slot, counts_ref, trace_ref, out_ref, rows_ref):
    step = pl.program_id(0)
    capacity = trace_ref.shape[0]
    top = capacity - slot - 16

    def skip(d, total):
        return total + counts_ref[d]

    start = lax.fori_loop(0, step * per_step, skip, jnp.int32(0))
    for i in range(per_step):
        base = pl.multiple_of(jnp.minimum(start // 16 * 16, top), 16)
        for j in range(2):
            half = slice(j * NU, (j + 1) * NU)
            rows_ref[i, j] = trace_ref[pl.ds(base, slot + 16), half].astype(jnp.float32)
            out_ref[i, :, half] = rows_ref[i, j, pl.ds(start - base, slot), :].astype(out_ref.dtype)
        start = start + counts_ref[step * per_step + i]


def pack(counts, trace, slots, slot):
    per_step = 4
    return pl.pallas_call(
        functools.partial(pack_kernel, per_step, slot),
        out_shape=jax.ShapeDtypeStruct((slots, slot, trace.shape[1]), trace.dtype),
        grid_spec=pltpu.PrefetchScalarGridSpec(
            num_scalar_prefetch=1,
            grid=(slots // per_step,),
            in_specs=[pl.BlockSpec(trace.shape, lambda i, c: (0, 0))],
            out_specs=pl.BlockSpec((per_step, slot, trace.shape[1]), lambda i, c: (i, 0, 0)),
            scratch_shapes=[pltpu.VMEM((per_step, 2, slot + 16, NU), jnp.float32)],
        ),
        name="pack_rows",
    )(counts, trace)


def unpack_kernel(per_step, counts_ref, recv_ref, sensor_ref, power_ref, rows_ref):
    step = pl.program_id(0)
    slot = recv_ref.shape[1]
    owned = power_ref.shape[0]

    def skip(s, total):
        return total + counts_ref[s]

    at = lax.fori_loop(0, step * per_step, skip, jnp.int32(0))
    for i in range(per_step):
        for j in range(2):
            half = recv_ref[i, :, j * NU:(j + 1) * NU]
            rows_ref[j, pl.ds(at, slot), :] = half.astype(jnp.float32)
        at = at + counts_ref[step * per_step + i]

    @pl.when(step == pl.num_programs(0) - 1)
    def _():
        def tile(k, carry):
            here = pl.multiple_of(k * 128, 128)
            power_ref[pl.ds(here, 128), :] = rows_ref[0, pl.ds(here, 128), :].astype(power_ref.dtype)
            block = rows_ref[1, pl.ds(here, 128), :]
            sensor_ref[:, pl.ds(here, 128)] = block.T.astype(sensor_ref.dtype)
            return carry

        lax.fori_loop(0, owned // 128, tile, 0)


def unpack(counts, recv, owned):
    per_step = 4
    slots, slot, width = recv.shape
    return pl.pallas_call(
        functools.partial(unpack_kernel, per_step),
        out_shape=(
            jax.ShapeDtypeStruct((NU, owned), recv.dtype),
            jax.ShapeDtypeStruct((owned, NU), recv.dtype),
        ),
        grid_spec=pltpu.PrefetchScalarGridSpec(
            num_scalar_prefetch=1,
            grid=(slots // per_step,),
            in_specs=[pl.BlockSpec((per_step, slot, width), lambda i, c: (i, 0, 0))],
            out_specs=(
                pl.BlockSpec((NU, owned), lambda i, c: (0, 0)),
                pl.BlockSpec((owned, NU), lambda i, c: (0, 0)),
            ),
            scratch_shapes=[pltpu.VMEM((2, owned + slot, NU), jnp.float32)],
        ),
        name="unpack_rows",
    )(counts, recv)


def corr_kernel(scale, sensor_ref, power_ref, out_ref, *scratch):
    (wide, landed, rows, shifted, head, ex_send, ex_recv, edge_send, edge_recv,
     rs_send, rs_recv) = scratch[:11]
    acc = scratch[11:17]
    got = scratch[17:23]
    owned = power_ref.shape[0]
    total = 2 * owned
    grp = lax.axis_index("grp")
    dev = lax.axis_index("dev")
    core = dev % 2
    chip = dev // 2
    y = chip % 4
    x = chip // 4
    partner = (grp, dev + 1 - 2 * core)
    after = (chip + 1) % 16
    before = (chip + 15) % 16

    def place(xx, yy, zz):
        return (zz, xx * 8 + yy * 2 + core)

    def near(a):
        return a + 1 - 2 * (a % 2)

    def far(a):
        return 3 - a

    neighbours = (
        place(near(x), y, grp), place(x, near(y), grp), place(x, y, near(grp)),
        place(far(x), y, grp), place(x, far(y), grp), place(x, y, far(grp)),
    )

    def near_bit(a):
        return (a // 2 + a % 2) % 2

    own_bits = (near_bit(x), near_bit(y), near_bit(grp), x // 2, y // 2, grp // 2)

    barrier = pltpu.get_barrier_semaphore()

    def greet(target):
        pl.semaphore_signal(barrier, inc=1, device_id=target, device_id_type=MESH)

    greet(partner)
    for target in neighbours:
        greet(target)
    greet((grp, before * 2 + 1))
    greet((grp, after * 2))
    greet((grp, jnp.where(core == 1, after * 2 + 1, before * 2)))
    pl.semaphore_wait(barrier, 10)

    own_at = pl.multiple_of(core * owned, 128)
    here = (
        (sensor_ref, wide.at[0:NU, pl.ds(own_at, owned)]),
        (power_ref, landed.at[pl.ds(pl.multiple_of(HALO + core * owned, 128), owned), :]),
    )
    exchange = [
        pltpu.make_async_remote_copy(
            src_ref=src, dst_ref=dst, send_sem=ex_send.at[i], recv_sem=ex_recv.at[i],
            device_id=partner, device_id_type=MESH)
        for i, (src, dst) in enumerate(here)
    ]
    edges = (
        (sensor_ref.at[:, 0:128], head, before),
        (power_ref.at[pl.ds(owned - HALO, HALO), :], landed.at[0:HALO, :], after),
    )

    def edge_copy(i, which):
        src, dst, target = edges[i]
        return pltpu.make_async_remote_copy(
            src_ref=src, dst_ref=dst, send_sem=edge_send.at[which], recv_sem=edge_recv.at[i],
            device_id=(grp, target * 2 + which), device_id_type=MESH)

    for i in range(2):
        @pl.when(core == i)
        def _(i=i):
            for which in range(2):
                edge_copy(i, which).start()

    for copy in exchange:
        copy.start()
    wide[0:NU, pl.ds(own_at, owned)] = sensor_ref[...]
    power_at = pl.multiple_of(HALO + core * owned, 128)
    rows[pl.ds(power_at, owned), :] = power_ref[...].astype(jnp.float32)
    exchange[1].wait_recv()
    other_at = pl.multiple_of(HALO + (1 - core) * owned, 128)
    rows[pl.ds(other_at, owned), :] = landed[pl.ds(other_at, owned), :].astype(jnp.float32)
    edge_copy(1, 0).wait_recv()
    rows[0:HALO, :] = jnp.where(chip > 0, landed[0:HALO, :].astype(jnp.float32), 0.0)

    def shift_rows(k, carry):
        at = pl.multiple_of(k * 912, 16)
        for u in range(4):
            shifted[u, pl.ds(at, 912), :] = rows[
                pl.ds(at + 16 - 4 * u - 2 * core, 912), :].astype(shifted.dtype)
        return carry

    lax.fori_loop(0, (LEAD + total) // 912, shift_rows, 0)

    edge_copy(0, 0).wait_recv()
    exchange[0].wait_recv()
    lane = lax.broadcasted_iota(jnp.int32, (NU, 128), 1)

    def turn(block):
        return pltpu.roll(block.astype(jnp.float32), 127, 1)

    def shift_lanes(k, following):
        at = pl.multiple_of(total - 128 - k * 128, 128)
        turned = turn(wide[0:NU, pl.ds(at, 128)])
        wide[NU:2 * NU, pl.ds(at, 128)] = jnp.where(lane == 127, following, turned).astype(wide.dtype)
        return turned

    lax.fori_loop(0, total // 128, shift_lanes, jnp.where(chip < 15, turn(head[...]), 0.0))

    def step_copy(step, q, src, dst):
        return pltpu.make_async_remote_copy(
            src_ref=src, dst_ref=dst, send_sem=rs_send.at[step, q], recv_sem=rs_recv.at[step, q],
            device_id=neighbours[(q + step) % DIMS], device_id_type=MESH)

    def read_at(bits):
        flip = [(o + b) % 2 for o, b in zip(own_bits, bits)]
        xd, yd, zd = (2 * flip[3 + i] + (flip[i] + flip[3 + i]) % 2 for i in range(3))
        return yd, pl.multiple_of(LEAD - 16 * (zd * 4 + xd), 16)

    def pair(i, carry):
        first = BLOCKS - 1 - 2 * i
        both = []
        for block in (first, first - 1):
            bits = [(block // 2 ** b) % 2 for b in range(DIMS)]
            both.append((bits, read_at(bits)))
        result = None
        for k in range(0, total, K_CHUNK):
            operand = jnp.concatenate(
                [shifted[u, pl.ds(at + k, K_CHUNK), :] for _, (u, at) in both], axis=1)
            term = jnp.dot(wide[:, k:k + K_CHUNK], operand, preferred_element_type=jnp.float32)
            result = term if result is None else result + term
        for j, (bits, _) in enumerate(both):
            for q in range(DIMS):
                index = sum(bits[(q + e) % DIMS] * 2 ** (DIMS - 1 - e) for e in range(DIMS))
                acc[q][index] = result[PART_AT[q]:PART_AT[q] + PARTS[q], j * NU:(j + 1) * NU]

                @pl.when(bits[q] == 1)
                def _(q=q, index=index):
                    step_copy(0, q, acc[q].at[index], got[q].at[index - BLOCKS // 2]).start()
        return carry

    lax.fori_loop(0, BLOCKS // 2, pair, 0)

    sent = [[step_copy(0, q, acc[q].at[32:64], got[q].at[0:32]) for q in range(DIMS)]]
    begin = 0
    for step in range(1, DIMS):
        n = 2 ** (DIMS - 1 - step)
        copies = []
        for q in range(DIMS):
            sent[step - 1][q].wait_recv()
            acc[q][n:2 * n] = acc[q][n:2 * n] + got[q][begin + n:begin + 2 * n]
            copy = step_copy(
                step, q, acc[q].at[n:2 * n], got[q].at[begin + 2 * n:begin + 3 * n])
            copy.start()
            copies.append(copy)
        for q in range(DIMS):
            acc[q][0:n] = acc[q][0:n] + got[q][begin:begin + n]
        sent.append(copies)
        begin += 2 * n
    for q in range(DIMS):
        sent[DIMS - 1][q].wait_recv()
        out_ref[PART_AT[q]:PART_AT[q] + PARTS[q], :] = (acc[q][0] + got[q][begin]) * scale

    for copies in sent:
        for copy in copies:
            copy.wait_send()
    for copy in exchange:
        copy.wait_send()

    for i in range(2):
        @pl.when(core == i)
        def _(i=i):
            for which in range(2):
                edge_copy(i, which).wait_send()


def correlate(sensor, power, scale):
    owned = power.shape[0]
    total = 2 * owned
    kind = power.dtype
    return pl.pallas_call(
        functools.partial(corr_kernel, scale),
        out_shape=jax.ShapeDtypeStruct((2 * NU, NU), jnp.float32),
        in_specs=[pl.BlockSpec(memory_space=pltpu.VMEM)] * 2,
        out_specs=pl.BlockSpec(memory_space=pltpu.VMEM),
        scratch_shapes=[
            pltpu.VMEM((2 * NU, total), kind),
            pltpu.VMEM((HALO + total, NU), kind),
            pltpu.VMEM((HALO + total, NU), jnp.float32),
            pltpu.VMEM((4, LEAD + total, NU), kind),
            pltpu.VMEM((NU, 128), kind),
            pltpu.SemaphoreType.DMA((2,)),
            pltpu.SemaphoreType.DMA((2,)),
            pltpu.SemaphoreType.DMA((2,)),
            pltpu.SemaphoreType.DMA((2,)),
            pltpu.SemaphoreType.DMA((DIMS, DIMS)),
            pltpu.SemaphoreType.DMA((DIMS, DIMS)),
        ]
        + [pltpu.VMEM((BLOCKS, h, NU), jnp.float32) for h in PARTS]
        + [pltpu.VMEM((BLOCKS - 1, h, NU), jnp.float32) for h in PARTS],
        compiler_params=pltpu.CompilerParams(
            collective_id=0, has_side_effects=True, vmem_limit_bytes=56 << 20),
        name="correlate_scatter",
    )(sensor, power)


def per_device(trace, counts):
    dev_count = lax.axis_size("dev")
    group_count = lax.axis_size("grp")
    capacity = trace.shape[0]
    slot_rows = capacity // dev_count
    owned = capacity // 2
    send_counts = counts.reshape(-1)
    recv_counts = lax.all_to_all(
        send_counts.reshape(dev_count, 1), "dev", split_axis=0, concat_axis=0, tiled=True
    ).reshape(-1)
    packed = pack(send_counts, trace, dev_count, slot_rows)
    received = lax.all_to_all(packed, "dev", split_axis=0, concat_axis=0, tiled=True)
    sensor, power = unpack(recv_counts, received, owned)
    scale = 1.0 / math.sqrt(group_count * dev_count * owned)
    return correlate(sensor, power, scale).reshape(2, NU, NU)


def solution(mesh):
    in_specs = (P(("grp", "dev"), None), P("grp", "dev", None))
    out_specs = P(("grp", "dev"), None, None)
    return jax.shard_map(
        per_device, mesh=mesh, in_specs=in_specs, out_specs=out_specs, check_vma=False
    )
```

time: 1640 us -> 160 us (0.10)
  local copies, waits for them, and re-layouts: 715 us -> 4.55 us
  waiting for transfers between devices: 713 us -> 39.9 us
  matrix products: 148 us -> 0 us
  Pallas kernels: 0 us -> 99.9 us
    reduce_scatter x1 -> x0, waiting for transfers between devices: 674 us -> none  [per_device(): lax.psum_scatter(all_terms, ('grp', 'dev'), scatter_dimension=0, tiled=True)]
    while x240 -> x0, local copies, waits for them, and re-layouts: 546 us -> none
    dot_general x16 -> x0, matrix products: 148 us -> none  [lag_block(): lax.dot_general(sensor, stacked, (((0,), (0,)), ((), ())), preferred_elem...]
    pallas_call x0 -> x3, Pallas kernels: none -> 99.9 us  [the longest x1 84.6 us: correlate(): pl.pallas_call(functools.partial(corr_kernel, scale), out_shape=jax.Shape...]
    dynamic_update_slice x32 -> x0, local copies, waits for them, and re-layouts: 78 us -> none  [per_device(): lax.map(lag_block, jnp.arange(lag_count // block_width, dtype=jnp.int32))]
    gather x2 -> x0, local copies, waits for them, and re-layouts: 39.3 us -> none  [the longest x1 24.9 us: per_device(): trace[row_index]]
    concatenate x16 -> x0, local copies, waits for them, and re-layouts: 36.4 us -> none  [lag_block(): jnp.concatenate([stretch[block_width - 1 - step:block_width - 1 - step +...]
  transfers between devices with their start and end apart: 4 -> 2, of which waited for: 2 -> 2; matrix products, arithmetic and copies ran while one was open for 2% -> 1% of each run, Pallas kernels for 0% -> 4%
where the time goes in v1:
time: 160 us; the launch traced here: 159 us
  Pallas kernels  99.9 us (62%)
  waiting for transfers between devices  39.9 us (25%)
  starting transfers between devices  13.9 us (9%)
  local copies, waits for them, and re-layouts  4.55 us (3%)
    pallas_call x1, Pallas kernels, correlate(): pl.pallas_call(functools.partial(corr_kernel, scale), out_shape=jax.Shape...  84.6 us
    all_to_all x1, waiting for transfers between devices, per_device(): lax.all_to_all(packed, 'dev', split_axis=0, concat_axis=0, tiled=True)  39 us
    pallas_call x1, Pallas kernels, unpack(): pl.pallas_call(functools.partial(unpack_kernel, per_step), out_shape=(jax...  8.81 us
    all_to_all x1, starting transfers between devices, per_device(): lax.all_to_all(send_counts.reshape(dev_count, 1), 'dev', split_axis=0, co...  7.43 us
    all_to_all x1, starting transfers between devices, per_device(): lax.all_to_all(packed, 'dev', split_axis=0, concat_axis=0, tiled=True)  6.47 us
    pallas_call x1, Pallas kernels, pack(): pl.pallas_call(functools.partial(pack_kernel, per_step, slot), out_shape=...  6.4 us
    unnamed x3, local copies, waits for them, and re-layouts  3.22 us
  transfers between devices with their start and end apart: 2, of which 2 were waited for; matrix products, arithmetic and copies ran while one was open for 1% of the time, Pallas kernels for 4%

profile of v1, /device:TPU:0, one launch (start us, length us, event | category | flops | bytes accessed | tf_op | source)
XLA Modules:
  0.0 159.4 jit_solution(14535392492543220149)
XLA Ops:
  0.0 1.3 copy.4
  1.3 7.4 %all-to-all-start = ((s32[32,1,1]{2,1,0:T(1,128)}), s32[32,1,1]{2,1,0:T(1,128)S(1)}, u32[]{:S(2)}, u32[]{:S(2)}) async-start(s32[32,1,1]{2,1,0:T(1,128)} %copy.4), calls=%async_computation | async-start | bytes 32768 | tf_op jit(solution)/shard_map/all_to_all | solution.py:323
  8.8 6.4 %pack_rows.1 = bf16[32,192,256]{2,1,0:T(8,128)(2,1)} custom-call(s32[32]{0:T(128)} %bitcast.5, bf16[6144,256]{1,0:T(8,128)(2,1)} %trace_ref.1), custom_call_target="tpu_custom_call" | custom-call | tf_op jit(solution)/shard_map/pack_rows/pallas_call | solution.py:43
  15.2 0.9 all-to-all-done
  16.1 6.5 %all-to-all-start.1 = ((bf16[32,192,256]{2,1,0:T(8,128)(2,1)}), bf16[32,192,256]{2,1,0:T(8,128)(2,1)S(1)}, u32[]{:S(2)}, u32[]{:S(2)}) async-start(bf16[32,192,256]{2,1,0:T(8,128)(2,1)} %pack_rows.1), calls=%async_computation.1 | async-start | bytes 6291456 | tf_op jit(solution)/shard_map/all_to_all | solution.py:327
  22.6 1.2 reduce.counts_ref
  23.8 39.0 %all-to-all-done.1.recv_ref = bf16[32,192,256]{2,1,0:T(8,128)(2,1)S(1)} async-done(((bf16[32,192,256]{2,1,0:T(8,128)(2,1)}), bf16[32,192,256]{2,1,0:T(8,128)(2,1)S(1)}, u32[]{:S(2)}, u32[]{:S(2)}) %all-to-all-start.1) | async-done | bytes 3145760 | tf_op jit(solution)/shard_map/all_to_all | solution.py:327
  62.7 0.0 copy-start
  62.7 1.6 %copy-done = bf16[32,192,256]{2,1,0:T(8,128)(2,1)} copy-done((bf16[32,192,256]{2,1,0:T(8,128)(2,1)}, bf16[32,192,256]{2,1,0:T(8,128)(2,1)S(1)}, u32[]{:S(2)}) %copy-start) | copy-done | bytes 3145752
  64.4 8.8 %unpack_rows.1 = (bf16[128,3072]{1,0:T(8,128)(2,1)}, bf16[3072,128]{1,0:T(8,128)(2,1)}) custom-call(s32[32]{0:T(128)} %reduce.counts_ref, bf16[32,192,256]{2,1,0:T(8,128)(2,1)} %copy-done), custom_call_target="tpu_custom_call" | custom-call | tf_op jit(solution)/shard_map/unpack_rows/pallas_call | solution.py:87
  73.2 84.6 %correlate_scatter.1 = f32[256,128]{1,0:T(8,128)} custom-call(bf16[128,3072]{1,0:T(8,128)(2,1)} %get-tuple-element.7.sensor_ref, bf16[3072,128]{1,0:T(8,128)(2,1)} %get-tuple-element.8.power_ref), custom_call_target="tpu_custom_call" | custom-call | tf_op jit(solution)/shard_map/correlate_scatter/pallas_call | solution.py:290
  157.8 1.6 copy.6
Async XLA Ops:
  1.3 14.8 %all-to-all-start = ((s32[32,1,1]{2,1,0:T(1,128)}), s32[32,1,1]{2,1,0:T(1,128)S(1)}, u32[]{:S(2)}, u32[]{:S(2)}) async-start(s32[32,1,1]{2,1,0:T(1,128)} %copy.4), calls=%async_computation | async-start | bytes 32768 | tf_op jit(solution)/shard_map/all_to_all | solution.py:323
  16.1 46.6 %all-to-all-start.1 = ((bf16[32,192,256]{2,1,0:T(8,128)(2,1)}), bf16[32,192,256]{2,1,0:T(8,128)(2,1)S(1)}, u32[]{:S(2)}, u32[]{:S(2)}) async-start(bf16[32,192,256]{2,1,0:T(8,128)(2,1)} %pack_rows.1), calls=%async_computation.1 | async-start | bytes 6291456 | tf_op jit(solution)/shard_map/all_to_all | solution.py:327
  62.7 1.6 %copy-start = (bf16[32,192,256]{2,1,0:T(8,128)(2,1)}, bf16[32,192,256]{2,1,0:T(8,128)(2,1)S(1)}, u32[]{:S(2)}) copy-start(bf16[32,192,256]{2,1,0:T(8,128)(2,1)S(1)} %all-to-all-done.1.recv_ref) | copy-start | bytes 9437188

commit v2 on v1

--- a/solution.py
+++ b/solution.py
@@ -52,6 +52,200 @@
         ),
         name="pack_rows",
     )(counts, trace)
+
+
+def exchange_kernel(lengths_ref, packed_ref, recv_ref, table_ref, mid, turn_first, turn_last,
+                    table_send, table_recv, send_sem, recv_sem, own_sem):
+    slots = table_ref.shape[0]
+    grp = lax.axis_index("grp")
+    dev = lax.axis_index("dev")
+    core = dev % 2
+    y = dev // 2 % 4
+    x = dev // 8
+    barrier = pltpu.get_barrier_semaphore()
+
+    def greet(k, carry):
+        pl.semaphore_signal(barrier, inc=1, device_id=(grp, (dev + k) % slots), device_id_type=MESH)
+        return carry
+
+    lax.fori_loop(1, slots, greet, 0)
+    used = []
+
+    def remote(src, dst, target):
+        i = len(used)
+        copy = pltpu.make_async_remote_copy(
+            src_ref=src, dst_ref=dst, send_sem=send_sem.at[i], recv_sem=recv_sem.at[i],
+            device_id=(grp, target), device_id_type=MESH)
+        used.append(copy)
+        return copy
+
+    def cell(ref, h, a, b, c):
+        return ref.at[a, b, c, h] if h == 0 else ref.at[b, a, c, h]
+
+    def block(h, a, c=slice(None)):
+        return packed_ref.at[a, :, c, h] if h == 0 else packed_ref.at[:, a, c, h]
+
+    at = ((x, y), (y, x))
+
+    def place(h, da, db, dc):
+        a = (at[h][0] + da) % 4
+        b = (at[h][1] + db) % 4
+        c = (core + dc) % 2
+        return a * 8 + b * 2 + c if h == 0 else b * 8 + a * 2 + c
+
+    def table_copy(k):
+        return pltpu.make_async_remote_copy(
+            src_ref=lengths_ref, dst_ref=table_ref.at[dev], send_sem=table_send.at[k],
+            recv_sem=table_recv.at[k], device_id=(grp, (dev + k) % slots), device_id_type=MESH)
+
+    ways = (1, 3)
+    halves = (0, 1)
+
+    def core_for(j):
+        return (core + j) % 2
+
+    far_first = {}
+    near_first = {}
+    far_second = {}
+    for j, way in enumerate(ways):
+        for h in halves:
+            far_first[h, j] = remote(
+                block(h, (at[h][0] + 2) % 4, core_for(j)), turn_first.at[h, j], place(h, way, 0, 0))
+    for j, way in enumerate(ways):
+        for h in halves:
+            near_first[h, j] = remote(
+                block(h, (at[h][0] + way) % 4), mid.at[h, 3 - way], place(h, way, 0, 0))
+    for j, way in enumerate(ways):
+        for h in halves:
+            far_second[h, j] = remote(
+                turn_first.at[h, j], mid.at[h, 1, :, core_for(j)], place(h, way, 0, 0))
+
+    def last(h, da):
+        a, b = at[h]
+        origin = (a + da) % 4
+
+        def held(db, c):
+            if da == 0:
+                return cell(packed_ref, h, a, (b + db) % 4, c)
+            return mid.at[h, da - 1, (b + db) % 4, c]
+
+        far = []
+        near = []
+        for j, way in enumerate(ways):
+            first = remote(held(2, core_for(j)), turn_last.at[h, j, da], place(h, 0, way, 0))
+            second = remote(
+                turn_last.at[h, j, da], cell(recv_ref, h, origin, (b - way) % 4, core),
+                place(h, 0, way, j))
+            far.append((first, second))
+        for way in ways:
+            for dc in range(2):
+                near.append(remote(
+                    held(way, core_for(dc)), cell(recv_ref, h, origin, b, core),
+                    place(h, 0, way, dc)))
+        near.append(remote(
+            held(0, core_for(1)), cell(recv_ref, h, origin, b, core), place(h, 0, 0, 1)))
+        own = pltpu.make_async_copy(
+            held(0, core), cell(recv_ref, h, origin, b, core), own_sem.at[h, da])
+        return far, near, own
+
+    second_stage = {(h, da): last(h, da) for da in range(4) for h in halves}
+    own_table = pltpu.make_async_copy(lengths_ref, table_ref.at[dev], own_sem.at[2, 0])
+    own_table.start()
+    pl.semaphore_wait(barrier, slots - 1)
+
+    for copy in far_first.values():
+        copy.start()
+    for copy in near_first.values():
+        copy.start()
+
+    def send_table(k, carry):
+        table_copy(k).start()
+        return carry
+
+    lax.fori_loop(1, slots, send_table, 0)
+
+    def begin(h, da):
+        far, near, own = second_stage[h, da]
+        for first, _ in far:
+            first.start()
+        for copy in near:
+            copy.start()
+        own.start()
+
+    def forward(h, da):
+        for first, second in second_stage[h, da][0]:
+            first.wait_recv()
+            second.start()
+
+    for key, copy in far_first.items():
+        copy.wait_recv()
+        far_second[key].start()
+    for h in halves:
+        begin(h, 0)
+    for j, way in enumerate(ways):
+        for h in halves:
+            near_first[h, j].wait_recv()
+            begin(h, 4 - way)
+    for h in halves:
+        forward(h, 0)
+    for h in halves:
+        for j in range(2):
+            far_second[h, j].wait_recv()
+        begin(h, 2)
+    for da in (3, 1, 2):
+        for h in halves:
+            forward(h, da)
+    for h in halves:
+        for da in range(4):
+            far, near, own = second_stage[h, da]
+            for _, second in far:
+                second.wait_recv()
+            for copy in near:
+                copy.wait_recv()
+            own.wait()
+    for copy in used:
+        copy.wait_send()
+    own_table.wait()
+
+    def finish(k, carry):
+        table_copy(k).wait()
+        return carry
+
+    lax.fori_loop(1, slots, finish, 0)
+
+
+def exchange(counts, packed):
+    slots, slot, width = packed.shape
+    half = slot // 2
+    kind = packed.dtype
+    lengths = jnp.broadcast_to(jnp.pad(counts, (0, 128 - slots)), (8, 128))
+    shape = (4, 4, 2, 2, half, width)
+    copies = 12 + 8 * 9
+    received, table = pl.pallas_call(
+        exchange_kernel,
+        out_shape=(
+            jax.ShapeDtypeStruct(shape, kind),
+            jax.ShapeDtypeStruct((slots, 8, 128), jnp.int32),
+        ),
+        in_specs=[
+            pl.BlockSpec(memory_space=pltpu.VMEM),
+            pl.BlockSpec(memory_space=pl.ANY),
+        ],
+        out_specs=(pl.BlockSpec(memory_space=pl.ANY), pl.BlockSpec(memory_space=pl.ANY)),
+        scratch_shapes=[
+            pltpu.VMEM((2, 3, 4, 2, half, width), kind),
+            pltpu.VMEM((2, 2, 4, half, width), kind),
+            pltpu.VMEM((2, 2, 4, half, width), kind),
+            pltpu.SemaphoreType.DMA((slots,)),
+            pltpu.SemaphoreType.DMA((slots,)),
+            pltpu.SemaphoreType.DMA((copies,)),
+            pltpu.SemaphoreType.DMA((copies,)),
+            pltpu.SemaphoreType.DMA((3, 4)),
+        ],
+        compiler_params=pltpu.CompilerParams(collective_id=1, has_side_effects=True),
+        name="ring_exchange",
+    )(lengths, packed.reshape(shape))
+    return received.reshape(slots, slot, width), table
 
 
 def unpack_kernel(per_step, counts_ref, recv_ref, sensor_ref, power_ref, rows_ref):
@@ -320,11 +514,8 @@
     slot_rows = capacity // dev_count
     owned = capacity // 2
     send_counts = counts.reshape(-1)
-    recv_counts = lax.all_to_all(
-        send_counts.reshape(dev_count, 1), "dev", split_axis=0, concat_axis=0, tiled=True
-    ).reshape(-1)
-    packed = pack(send_counts, trace, dev_count, slot_rows)
-    received = lax.all_to_all(packed, "dev", split_axis=0, concat_axis=0, tiled=True)
+    received, table = exchange(send_counts, pack(send_counts, trace, dev_count, slot_rows))
+    recv_counts = lax.dynamic_index_in_dim(table[:, 0, :], lax.axis_index("dev"), 1, False)
     sensor, power = unpack(recv_counts, received, owned)
     scale = 1.0 / math.sqrt(group_count * dev_count * owned)
     return correlate(sensor, power, scale).reshape(2, NU, NU)

time: 160 us -> 152 us (0.950)
  Pallas kernels: 99.9 us -> 146 us
  waiting for transfers between devices: 39.9 us -> 0 us
  starting transfers between devices: 13.9 us -> 0 us
    pallas_call x0 -> x1, Pallas kernels: none -> 46.6 us  [exchange(): pl.pallas_call(exchange_kernel, out_shape=(jax.ShapeDtypeStruct(shape, ki...]
    all_to_all x2 -> x0, waiting for transfers between devices: 39.9 us -> none  [the longest x1 39 us: per_device(): lax.all_to_all(packed, 'dev', split_axis=0, concat_axis=0, tiled=True)]
    all_to_all x2 -> x0, starting transfers between devices: 13.9 us -> none  [the longest x1 7.43 us: per_device(): lax.all_to_all(send_counts.reshape(dev_count, 1), 'dev', split_axis=0, co...]
    unnamed x3 -> x1, local copies, waits for them, and re-layouts: 3.22 us -> 1.57 us
  transfers between devices with their start and end apart: 2 -> 0, of which waited for: 2 -> 0; matrix products, arithmetic and copies ran while one was open for 1% -> 0% of each run, Pallas kernels for 4% -> 0%
where the time goes in v2:
time: 152 us; the launch traced here: 151 us
  Pallas kernels  146 us (96%)
  local copies, waits for them, and re-layouts  4.99 us (3%)
    pallas_call x1, Pallas kernels, correlate(): pl.pallas_call(functools.partial(corr_kernel, scale), out_shape=jax.Shape...  84.5 us
    pallas_call x1, Pallas kernels, exchange(): pl.pallas_call(exchange_kernel, out_shape=(jax.ShapeDtypeStruct(shape, ki...  46.6 us
    pallas_call x1, Pallas kernels, unpack(): pl.pallas_call(functools.partial(unpack_kernel, per_step), out_shape=(jax...  8.8 us
    pallas_call x1, Pallas kernels, pack(): pl.pallas_call(functools.partial(pack_kernel, per_step, slot), out_shape=...  6.38 us

profile of v2, /device:TPU:0, one launch (start us, length us, event | category | flops | bytes accessed | tf_op | source)
XLA Modules:
  0.0 151.3 jit_solution(17303148411236567047)
XLA Ops:
  0.0 0.7 pad.4
  0.7 0.6 broadcast_in_dim.3.lengths_ref
  1.3 6.4 %pack_rows.1 = bf16[32,192,256]{2,1,0:T(8,128)(2,1)} custom-call(s32[32]{0:T(128)} %bitcast.8, bf16[6144,256]{1,0:T(8,128)(2,1)} %trace_ref.1), custom_call_target="tpu_custom_call" | custom-call | tf_op jit(solution)/shard_map/pack_rows/pallas_call | solution.py:43
  7.6 46.6 %ring_exchange.1 = (bf16[4,4,2,2,96,256]{5,4,3,2,1,0:T(8,128)(2,1)}, s32[32,8,128]{2,1,0:T(8,128)}) custom-call(s32[8,128]{1,0:T(8,128)} %broadcast_in_dim.3.lengths_ref, bf16[4,4,2,2,96,256]{5,4,3,2,1,0:T(8,128)(2,1)} %bitcast.4), custom_call_target="tpu_custom_call" | custom-call | tf_op jit(solution)/shard_map/ring_exchange/pallas_call | solution.py:224
  54.2 0.9 slice.3
  55.1 1.2 dynamic-slice_reduce_fusion.counts_ref
  56.4 8.8 %unpack_rows.1 = (bf16[128,3072]{1,0:T(8,128)(2,1)}, bf16[3072,128]{1,0:T(8,128)(2,1)}) custom-call(s32[32]{0:T(128)} %dynamic-slice_reduce_fusion.counts_ref, bf16[32,192,256]{2,1,0:T(8,128)(2,1)} %bitcast.5), custom_call_target="tpu_custom_call" | custom-call | tf_op jit(solution)/shard_map/unpack_rows/pallas_call | solution.py:281
  65.2 84.5 %correlate_scatter.1 = f32[256,128]{1,0:T(8,128)} custom-call(bf16[128,3072]{1,0:T(8,128)(2,1)} %get-tuple-element.11.sensor_ref, bf16[3072,128]{1,0:T(8,128)(2,1)} %get-tuple-element.12.power_ref), custom_call_target="tpu_custom_call" | custom-call | tf_op jit(solution)/shard_map/correlate_scatter/pallas_call | solution.py:484
  149.7 1.6 %copy.4 = f32[2,128,128]{2,1,0:T(8,128)} copy(f32[2,128,128]{2,1,0:T(8,128)} %bitcast.6) | data formatting | bytes 262144

commit v3 on v2

--- a/solution.py
+++ b/solution.py
@@ -18,6 +18,7 @@
 PARTS = (48, 40, 40, 48, 40, 40)
 PART_AT = (0, 48, 88, 128, 176, 216)
 K_CHUNK = 2048
+BEHIND = 5
 
 
 def pack_kernel(per_step, slot, counts_ref, trace_ref, out_ref, rows_ref):
@@ -300,9 +301,9 @@
 
 def corr_kernel(scale, sensor_ref, power_ref, out_ref, *scratch):
     (wide, landed, rows, shifted, head, ex_send, ex_recv, edge_send, edge_recv,
-     rs_send, rs_recv) = scratch[:11]
-    acc = scratch[11:17]
-    got = scratch[17:23]
+     rs_send, rs_recv, first_recv) = scratch[:12]
+    acc = scratch[12:18]
+    got = scratch[18:24]
     owned = power_ref.shape[0]
     total = 2 * owned
     grp = lax.axis_index("grp")
@@ -420,33 +421,94 @@
         xd, yd, zd = (2 * flip[3 + i] + (flip[i] + flip[3 + i]) % 2 for i in range(3))
         return yd, pl.multiple_of(LEAD - 16 * (zd * 4 + xd), 16)
 
+    def first_copy(q, index):
+        slot = index % (BLOCKS // 2)
+        return pltpu.make_async_remote_copy(
+            src_ref=acc[q].at[slot + BLOCKS // 2], dst_ref=got[q].at[slot],
+            send_sem=rs_send.at[0, q], recv_sem=first_recv.at[q, slot],
+            device_id=neighbours[q], device_id_type=MESH)
+
+    def bits_of(i):
+        first = BLOCKS - 1 - 2 * i
+        return [
+            [1 - j] + [(first // 2 ** b) % 2 for b in range(1, DIMS)] for j in range(2)]
+
+    def index_of(q, bits):
+        return sum(bits[(q + e) % DIMS] * 2 ** (DIMS - 1 - e) for e in range(DIMS))
+
+    def follow(i):
+        both = bits_of(i)
+
+        def take(q, j):
+            index = index_of(q, both[j]) % (BLOCKS // 2)
+            first_copy(q, index).wait_recv()
+            acc[q][index] = acc[q][index] + got[q][index]
+            return index
+
+        def pass_on(q, index):
+            low = index % (BLOCKS // 4)
+            step_copy(
+                1, q, acc[q].at[low + BLOCKS // 4], got[q].at[low + BLOCKS // 2]).start()
+
+        for q in range(DIMS):
+            which = (1,) if q == 0 else (0, 1)
+
+            def step(q=q, which=which):
+                taken = [take(q, j) for j in which]
+                if q == DIMS - 1:
+                    pass_on(q, taken[0])
+                else:
+                    @pl.when(both[0][q + 1] == 1)
+                    def _():
+                        for index in taken:
+                            pass_on(q, index)
+
+            if q == 0:
+                step()
+            else:
+                pl.when(both[0][q] == 0)(step)
+
     def pair(i, carry):
-        first = BLOCKS - 1 - 2 * i
-        both = []
-        for block in (first, first - 1):
-            bits = [(block // 2 ** b) % 2 for b in range(DIMS)]
-            both.append((bits, read_at(bits)))
+        both = bits_of(i)
+        reads = [read_at(bits) for bits in both]
         result = None
         for k in range(0, total, K_CHUNK):
             operand = jnp.concatenate(
-                [shifted[u, pl.ds(at + k, K_CHUNK), :] for _, (u, at) in both], axis=1)
+                [shifted[u, pl.ds(at + k, K_CHUNK), :] for u, at in reads], axis=1)
             term = jnp.dot(wide[:, k:k + K_CHUNK], operand, preferred_element_type=jnp.float32)
             result = term if result is None else result + term
-        for j, (bits, _) in enumerate(both):
-            for q in range(DIMS):
-                index = sum(bits[(q + e) % DIMS] * 2 ** (DIMS - 1 - e) for e in range(DIMS))
-                acc[q][index] = result[PART_AT[q]:PART_AT[q] + PARTS[q], j * NU:(j + 1) * NU]
-
-                @pl.when(bits[q] == 1)
-                def _(q=q, index=index):
-                    step_copy(0, q, acc[q].at[index], got[q].at[index - BLOCKS // 2]).start()
+        for q in range(DIMS):
+            for j in range(2):
+                acc[q][index_of(q, both[j])] = result[
+                    PART_AT[q]:PART_AT[q] + PARTS[q], j * NU:(j + 1) * NU]
+            if q == 0:
+                first_copy(q, index_of(q, both[0])).start()
+            else:
+                @pl.when(both[0][q] == 1)
+                def _(q=q):
+                    for j in range(2):
+                        first_copy(q, index_of(q, both[j])).start()
+
+        @pl.when(i >= BEHIND)
+        def _():
+            follow(i - BEHIND)
+
         return carry
 
     lax.fori_loop(0, BLOCKS // 2, pair, 0)
 
-    sent = [[step_copy(0, q, acc[q].at[32:64], got[q].at[0:32]) for q in range(DIMS)]]
-    begin = 0
-    for step in range(1, DIMS):
+    def rest(i, carry):
+        follow(i)
+        return carry
+
+    lax.fori_loop(BLOCKS // 2 - BEHIND, BLOCKS // 2, rest, 0)
+
+    sent = [
+        [step_copy(0, q, acc[q].at[32:64], got[q].at[0:32]) for q in range(DIMS)],
+        [step_copy(1, q, acc[q].at[16:32], got[q].at[32:48]) for q in range(DIMS)],
+    ]
+    begin = BLOCKS // 2
+    for step in range(2, DIMS):
         n = 2 ** (DIMS - 1 - step)
         copies = []
         for q in range(DIMS):
@@ -498,6 +560,7 @@
             pltpu.SemaphoreType.DMA((2,)),
             pltpu.SemaphoreType.DMA((DIMS, DIMS)),
             pltpu.SemaphoreType.DMA((DIMS, DIMS)),
+            pltpu.SemaphoreType.DMA((DIMS, BLOCKS // 2)),
         ]
         + [pltpu.VMEM((BLOCKS, h, NU), jnp.float32) for h in PARTS]
         + [pltpu.VMEM((BLOCKS - 1, h, NU), jnp.float32) for h in PARTS],

time: 152 us -> 148 us (0.974)
  Pallas kernels: 146 us -> 143 us
    pallas_call x1, Pallas kernels: 84.5 us -> 80.9 us  [correlate(): pl.pallas_call(functools.partial(corr_kernel, scale), out_shape=jax.Shape...]
where the time goes in v3:
time: 148 us
  Pallas kernels  143 us (97%)
  local copies, waits for them, and re-layouts  4.99 us (3%)
    pallas_call x1, Pallas kernels, correlate(): pl.pallas_call(functools.partial(corr_kernel, scale), out_shape=jax.Shape...  80.9 us
    pallas_call x1, Pallas kernels, exchange(): pl.pallas_call(exchange_kernel, out_shape=(jax.ShapeDtypeStruct(shape, ki...  46.6 us
    pallas_call x1, Pallas kernels, unpack(): pl.pallas_call(functools.partial(unpack_kernel, per_step), out_shape=(jax...  8.8 us
    pallas_call x1, Pallas kernels, pack(): pl.pallas_call(functools.partial(pack_kernel, per_step, slot), out_shape=...  6.38 us

profile of v3, /device:TPU:0, one launch (start us, length us, event | category | flops | bytes accessed | tf_op | source)
XLA Modules:
  0.0 147.7 jit_solution(5674853551509471127)
XLA Ops:
  0.0 0.7 pad.4
  0.7 0.6 broadcast_in_dim.3.lengths_ref
  1.3 6.4 %pack_rows.1 = bf16[32,192,256]{2,1,0:T(8,128)(2,1)} custom-call(s32[32]{0:T(128)} %bitcast.8, bf16[6144,256]{1,0:T(8,128)(2,1)} %trace_ref.1), custom_call_target="tpu_custom_call" | custom-call | tf_op jit(solution)/shard_map/pack_rows/pallas_call | solution.py:44
  7.6 46.6 %ring_exchange.1 = (bf16[4,4,2,2,96,256]{5,4,3,2,1,0:T(8,128)(2,1)}, s32[32,8,128]{2,1,0:T(8,128)}) custom-call(s32[8,128]{1,0:T(8,128)} %broadcast_in_dim.3.lengths_ref, bf16[4,4,2,2,96,256]{5,4,3,2,1,0:T(8,128)(2,1)} %bitcast.4), custom_call_target="tpu_custom_call" | custom-call | tf_op jit(solution)/shard_map/ring_exchange/pallas_call | solution.py:225
  54.2 0.9 slice.3
  55.1 1.2 dynamic-slice_reduce_fusion.counts_ref
  56.4 8.8 %unpack_rows.1 = (bf16[128,3072]{1,0:T(8,128)(2,1)}, bf16[3072,128]{1,0:T(8,128)(2,1)}) custom-call(s32[32]{0:T(128)} %dynamic-slice_reduce_fusion.counts_ref, bf16[32,192,256]{2,1,0:T(8,128)(2,1)} %bitcast.5), custom_call_target="tpu_custom_call" | custom-call | tf_op jit(solution)/shard_map/unpack_rows/pallas_call | solution.py:282
  65.2 80.9 %correlate_scatter.1 = f32[256,128]{1,0:T(8,128)} custom-call(bf16[128,3072]{1,0:T(8,128)(2,1)} %get-tuple-element.11.sensor_ref, bf16[3072,128]{1,0:T(8,128)(2,1)} %get-tuple-element.12.power_ref), custom_call_target="tpu_custom_call" | custom-call | tf_op jit(solution)/shard_map/correlate_scatter/pallas_call | solution.py:546
  146.1 1.6 %copy.4 = f32[2,128,128]{2,1,0:T(8,128)} copy(f32[2,128,128]{2,1,0:T(8,128)} %bitcast.6) | data formatting | bytes 262144

commit v4 on v3

--- a/solution.py
+++ b/solution.py
@@ -18,7 +18,7 @@
 PARTS = (48, 40, 40, 48, 40, 40)
 PART_AT = (0, 48, 88, 128, 176, 216)
 K_CHUNK = 2048
-BEHIND = 5
+BEHIND = 8
 
 
 def pack_kernel(per_step, slot, counts_ref, trace_ref, out_ref, rows_ref):

time: 148 us -> 148 us (level)
  no operation moved by 1% of the time
where the time goes in v4:
time: 148 us
  Pallas kernels  143 us (97%)
  local copies, waits for them, and re-layouts  4.99 us (3%)
    pallas_call x1, Pallas kernels, correlate(): pl.pallas_call(functools.partial(corr_kernel, scale), out_shape=jax.Shape...  80.8 us
    pallas_call x1, Pallas kernels, exchange(): pl.pallas_call(exchange_kernel, out_shape=(jax.ShapeDtypeStruct(shape, ki...  46.6 us
    pallas_call x1, Pallas kernels, unpack(): pl.pallas_call(functools.partial(unpack_kernel, per_step), out_shape=(jax...  8.8 us
    pallas_call x1, Pallas kernels, pack(): pl.pallas_call(functools.partial(pack_kernel, per_step, slot), out_shape=...  6.38 us

profile of v4, /device:TPU:0, one launch (start us, length us, event | category | flops | bytes accessed | tf_op | source)
XLA Modules:
  0.0 147.6 jit_solution(6103764803450165984)
XLA Ops:
  0.0 0.7 pad.4
  0.7 0.6 broadcast_in_dim.3.lengths_ref
  1.3 6.4 %pack_rows.1 = bf16[32,192,256]{2,1,0:T(8,128)(2,1)} custom-call(s32[32]{0:T(128)} %bitcast.8, bf16[6144,256]{1,0:T(8,128)(2,1)} %trace_ref.1), custom_call_target="tpu_custom_call" | custom-call | tf_op jit(solution)/shard_map/pack_rows/pallas_call | solution.py:44
  7.6 46.6 %ring_exchange.1 = (bf16[4,4,2,2,96,256]{5,4,3,2,1,0:T(8,128)(2,1)}, s32[32,8,128]{2,1,0:T(8,128)}) custom-call(s32[8,128]{1,0:T(8,128)} %broadcast_in_dim.3.lengths_ref, bf16[4,4,2,2,96,256]{5,4,3,2,1,0:T(8,128)(2,1)} %bitcast.4), custom_call_target="tpu_custom_call" | custom-call | tf_op jit(solution)/shard_map/ring_exchange/pallas_call | solution.py:225
  54.2 0.9 slice.3
  55.1 1.2 dynamic-slice_reduce_fusion.counts_ref
  56.4 8.8 %unpack_rows.1 = (bf16[128,3072]{1,0:T(8,128)(2,1)}, bf16[3072,128]{1,0:T(8,128)(2,1)}) custom-call(s32[32]{0:T(128)} %dynamic-slice_reduce_fusion.counts_ref, bf16[32,192,256]{2,1,0:T(8,128)(2,1)} %bitcast.5), custom_call_target="tpu_custom_call" | custom-call | tf_op jit(solution)/shard_map/unpack_rows/pallas_call | solution.py:282
  65.2 80.8 %correlate_scatter.1 = f32[256,128]{1,0:T(8,128)} custom-call(bf16[128,3072]{1,0:T(8,128)(2,1)} %get-tuple-element.11.sensor_ref, bf16[3072,128]{1,0:T(8,128)(2,1)} %get-tuple-element.12.power_ref), custom_call_target="tpu_custom_call" | custom-call | tf_op jit(solution)/shard_map/correlate_scatter/pallas_call | solution.py:546
  146.0 1.6 %copy.4 = f32[2,128,128]{2,1,0:T(8,128)} copy(f32[2,128,128]{2,1,0:T(8,128)} %bitcast.6) | data formatting | bytes 262144
